TPU v7x, 32 devices: a whole 2x2x4 slice. The times are simulated.
32 devices in a mesh: bond: 8 (over z, x), mpo: 4 (over y, core).
Axes of the slice: x: 2, y: 2, z: 4, core: 2. Of those that a mesh axis runs over, the one named last changes fastest.
Arguments:
- wave_blocks: bfloat16 [8, 16, 256, 256], P('bond'), may hold values from -6 to 6
- left_environment: bfloat16 [8, 8, 256, 256], P('mpo', 'bond'), may hold values from -0.375 to 0.375
- right_environment: bfloat16 [8, 8, 256, 256], P('mpo', 'bond'), may hold values from -0.375 to 0.375
- site_operators: bfloat16 [8, 16, 16], P('mpo'), may hold values from -1.1953125 to 1.1953125
- right_sector: int32 [8, 16, 1], P('bond'), may hold values from 0 to 7; in each aligned block of 16 rows (0 to 15, 16 to 31, ..., all dimensions but the last counted through in order) at most 2 rows name the same one
- left_sizes: int32 [8], replicated, may hold values from 128 to 256
- right_sizes: int32 [8], replicated, may hold values from 128 to 256
- sector_place: int32 [8], replicated, may hold values from 0 to 7, each once
Outputs:
- applied: bfloat16 [8, 16, 256, 256], P('bond', 'mpo')
Inputs may be any that keep to these rules, and one draw needn't show every extreme that they name: `right_sector`: among the 16 blocks of one bond index no right sector is named more than 2 times, a bound that some block reaches. `sector_place`: every position is taken by exactly one right sector.
All inputs are finite; a program needn't handle non-finite values.
Results may differ from a plain program's by a relative error of at most 0.0057.
Values may be sent and summed in bfloat16 or wider, within the bound.
A program may use at most 64 MiB of HBM per device.

v0:
```python
import jax
import jax.numpy as jnp
from jax import lax
from jax.sharding import PartitionSpec as P


def lookup(entries, indices):
    count = entries.shape[0]
    matches = indices[..., None] == jnp.arange(count, dtype=jnp.int32)
    return jnp.sum(jnp.where(matches, entries, 0), axis=-1)


def shards(
    wave_blocks,
    left_environment,
    right_environment,
    site_operators,
    right_sector,
    left_sizes,
    right_sizes,
    sector_place,
):
    sectors = wave_blocks.shape[0]
    states = wave_blocks.shape[1]
    block_rows = wave_blocks.shape[2]
    channels = left_environment.shape[0]
    first_sector = lax.axis_index("bond") * sectors
    sector_ids = right_sector[:, :, 0]
    offsets = jnp.arange(block_rows, dtype=jnp.int32)
    left_live = lax.dynamic_slice_in_dim(left_sizes, first_sector, sectors)
    row_mask = offsets[None, :] < left_live[:, None]
    column_mask = offsets[None, None, :] < lookup(right_sizes, sector_ids)[:, :, None]
    live_mask = row_mask[:, None, :, None] & column_mask[:, :, None, :]
    masked = jnp.where(live_mask, wave_blocks, jnp.zeros((), jnp.bfloat16))
    block_count = sectors * states
    flat_blocks = masked.reshape(block_count, block_rows, block_rows)
    place_flat = lookup(sector_place, sector_ids).reshape(block_count)
    gathered = lax.all_gather(right_environment, "bond", axis=1, tiled=True)
    chosen = jnp.take(gathered, place_flat, axis=1)
    right_part = jnp.einsum(
        "bac,hbxc->bhax", flat_blocks, chosen, preferred_element_type=jnp.float32
    ).astype(jnp.bfloat16)
    right_part = right_part.reshape(sectors, states, channels, block_rows, block_rows)
    same_sector = sector_ids[:, :, None] == sector_ids[:, None, :]
    mixing = jnp.where(same_sector[:, None], site_operators[None], jnp.zeros((), jnp.bfloat16))
    mixed = jnp.einsum(
        "nhst,nthac->nshac", mixing, right_part, preferred_element_type=jnp.float32
    ).astype(jnp.bfloat16)
    partial_value = jnp.einsum(
        "hnab,nshbc->nsac", left_environment, mixed, preferred_element_type=jnp.float32
    )
    per_device = states // lax.axis_size("mpo")
    first_state = lax.axis_index("mpo") * per_device
    summed = lax.psum(partial_value, "mpo")
    summed = lax.dynamic_slice_in_dim(summed, first_state, per_device, 1)
    kept_mask = lax.dynamic_slice_in_dim(live_mask, first_state, per_device, 1)
    return jnp.where(kept_mask, summed, jnp.zeros((), jnp.float32)).astype(jnp.bfloat16)


def solution(mesh):
    placed = (
        P("bond", None, None, None),
        P("mpo", "bond", None, None),
        P("mpo", "bond", None, None),
        P("mpo", None, None),
        P("bond", None, None),
        P(),
        P(),
        P(),
    )
    return jax.shard_map(
        shards, mesh=mesh, in_specs=placed, out_specs=P("bond", "mpo", None, None), check_vma=False
    )
```

profile of v0, /device:TPU:0, one launch (start us, length us, event | category | flops | bytes accessed | tf_op | source)
XLA Modules:
  0.0 172.7 jit_solution(5104987714782508854)
XLA Ops:
  6.5 0.0 copy-start
  6.5 0.0 copy-start.5
  6.5 0.0 copy-start.2
  6.5 0.0 copy-start.3
  6.5 0.0 copy-start.4
  6.5 0.0 all-gather.2.cloned.1.call-start
  6.6 0.7 all-gather.2.cloned.1.call-update
  7.3 2.9 %copy.12 = bf16[1,16,256,256]{2,3,1,0:T(8,128)(2,1)S(1)} copy(bf16[1,16,256,256]{3,2,1,0:T(8,128)(2,1)} %param.8) | data formatting | bytes 4194304 | tf_op args[0]
  10.2 0.0 copy-done.5
  10.2 0.6 dynamic_slice.9
  10.8 0.6 iota_compare_fusion.2
  11.4 0.0 copy-done.2
  11.4 0.0 copy-done.3
  11.4 0.0 copy-done.4
  11.4 0.1 select_reduce_fusion.1
  11.6 0.1 broadcast_compare_fusion
  11.6 0.1 iota_compare_fusion
  11.7 2.0 %broadcast_and_fusion = pred[1,16,256,256]{2,3,1,0:T(8,128)(4,1)} fusion(pred[16,256]{1,0:T(8,128)(4,1)S(1)} %iota_compare_fusion, pred[256]{0:T(512)(128)(4,1)S(1)} %iota_compare_fusion.2), kind=kLoop, calls=%fused_computation.15 | loop fusion | flops 1048576 | bytes 1052928 | tf_op jit(solution)/shard_map/and | solution.py:33
  13.7 47.6 %all-gather.2.cloned.1.call-done = bf16[2,8,256,256]{3,2,1,0:T(8,128)(2,1)} async-done(((bf16[2,1,256,256]{3,2,1,0:T(8,128)(2,1)}), bf16[2,8,256,256]{3,2,1,0:T(8,128)(2,1)}) %all-gather.2.cloned.1.call-update) | async-done | bytes 2097168 | tf_op jit(solution)/shard_map/all_gather | solution.py:38
  61.4 4.3 %gather_fusion = bf16[16,2,256,256]{3,2,1,0:T(8,128)(2,1)} fusion(bf16[2,8,256,256]{3,2,1,0:T(8,128)(2,1)} %all-gather.2.cloned.1.call-done, s32[1024]{0:T(1024)S(1)} %pad_clamp_fusion), kind=kCustom, calls=%fused_computation | custom fusion | bytes 8388672 | tf_op jit(solution)/shard_map/jit(_take)/gather | solution.py:39
  65.7 4.7 %fusion.2 = bf16[16,2,256,256]{3,2,1,0:T(8,128)(2,1)} fusion(bf16[16,2,256,256]{3,2,1,0:T(8,128)(2,1)} %gather_fusion, pred[16]{0:T(512)(128)(4,1)S(1)} %compare_and_fusion, bf16[1,16,256,256]{2,3,1,0:T(8,128)(2,1)S(1)} %copy.12, pred[16,256]{1,0:T(8,128)(4,1)S(1)} %iota_compare_fusion, pred[256]{0:T(512)(128)(4,1)S(1)} %iota_compare_fusion.2), kind=kOutput, calls=%fused_computation.3 | convolution fusion | flops 1077936128 | bytes 10490128 | tf_op jit(solution)/shard_map/bac,hbxc->bhax/dot_general | solution.py:40
  70.4 0.0 copy-start.1
  70.4 7.9 %copy.16 = bf16[16,2,256,256]{2,0,3,1:T(8,128)(2,1)} copy(bf16[16,2,256,256]{3,2,1,0:T(8,128)(2,1)} %fusion.2) | data formatting | bytes 8388608 | tf_op jit(solution)/shard_map/bac,hbxc->bhax/dot_general | solution.py:40
  78.3 0.0 copy-done.1
  78.3 3.4 %convert_bitcast_fusion = bf16[16,2,256,256]{3,0,2,1:T(8,128)(2,1)S(1)} fusion(bf16[16,2,256,256]{2,0,3,1:T(8,128)(2,1)} %copy.16, bf16[2,16,16]{2,1,0:T(8,128)(2,1)S(1)} %copy-done.1, pred[16,16]{1,0:T(8,128)(4,1)S(1)} %broadcast_compare_fusion), kind=kOutput, calls=%fused_computation.8 | convolution fusion | flops 69206528 | bytes 8389888 | tf_op jit(solution)/shard_map/nhst,nthac->nshac/dot_general | solution.py:46
  81.7 0.0 copy-done
  81.7 6.1 %fusion.11 = f32[1,16,256,256]{2,3,1,0:T(8,128)} fusion(bf16[16,2,256,256]{3,0,2,1:T(8,128)(2,1)S(1)} %convert_bitcast_fusion, bf16[2,1,256,256]{3,2,1,0:T(8,128)(2,1)S(1)} %copy-done), kind=kOutput, calls=%fused_computation.11 | convolution fusion | flops 1073741824 | bytes 8650752 | tf_op jit(solution)/shard_map/hnab,nshbc->nsac/dot_general | solution.py:49
  87.8 75.9 %all-reduce.1 = bf16[1,16,256,256]{2,3,1,0:T(8,128)(2,1)S(1)} all-reduce(f32[1,16,256,256]{2,3,1,0:T(8,128)} %fusion.11), channel_id=1, replica_groups=mesh['bond'=8,'mpo'=4] {'mpo'}, use_global_device_ids=true, to_apply=%region_2.3 | all-reduce | flops 1048576 | bytes 6291456 | tf_op jit(solution)/shard_map/psum | solution.py:54
  163.7 1.1 select_convert_fusion
  164.8 1.0 copy.14
  (3 shorter events, 0.0 us)
Async XLA Ops:
  6.5 75.1 %copy-start = (bf16[2,1,256,256]{3,2,1,0:T(8,128)(2,1)S(1)}, bf16[2,1,256,256]{3,2,1,0:T(8,128)(2,1)}, u32[]{:S(2)}) copy-start(bf16[2,1,256,256]{3,2,1,0:T(8,128)(2,1)} %param.9) | copy-start | bytes 786436
  6.5 3.6 %copy-start.5 = (s32[8]{0:T(128)S(1)}, s32[8]{0:T(128)}, u32[]{:S(2)}) copy-start(s32[8]{0:T(128)} %param.13) | copy-start | bytes 100
  6.5 4.9 %copy-start.2 = (s32[1,16,1]{1,2,0:T(1,128)S(1)}, s32[1,16,1]{1,2,0:T(1,128)}, u32[]{:S(2)}) copy-start(s32[1,16,1]{1,2,0:T(1,128)} %param.12) | copy-start | bytes 196
  6.5 4.9 %copy-start.3 = (s32[8]{0:T(128)S(1)}, s32[8]{0:T(128)}, u32[]{:S(2)}) copy-start(s32[8]{0:T(128)} %param.14) | copy-start | bytes 100
  6.5 4.9 %copy-start.4 = (s32[8]{0:T(128)S(1)}, s32[8]{0:T(128)}, u32[]{:S(2)}) copy-start(s32[8]{0:T(128)} %param.15) | copy-start | bytes 100
  6.5 54.8 %all-gather.2.cloned.1.call-start = ((), (), s32[]{:S(2)}) async-start(), calls=%async_computation | async-start | bytes 2359296 | tf_op jit(solution)/shard_map/all_gather | solution.py:38
  70.4 7.9 %copy-start.1 = (bf16[2,16,16]{2,1,0:T(8,128)(2,1)S(1)}, bf16[2,16,16]{2,1,0:T(8,128)(2,1)}, u32[]{:S(2)}) copy-start(bf16[2,16,16]{2,1,0:T(8,128)(2,1)} %param.11) | copy-start | bytes 3076
Sparse Core Ops, SparseCore 0:
  9.5 51.7 all-gather.1
where the time goes:
time: 173 us
  blocking collectives  75.9 us (44%)
  waiting for transfers between devices  48.3 us (28%)
  local copies, waits for them, and re-layouts  16.7 us (10%)
  matrix products  14.2 us (8%)
  between operations  13.5 us (8%)
  other arithmetic  4.04 us (2%)
    psum x1, blocking collectives, shards(): summed = lax.psum(partial_value, 'mpo')  75.9 us
    all_gather x1, waiting for transfers between devices, shards(): gathered = lax.all_gather(right_environment, 'bond', axis=1, tiled=True)  47.6 us
    dot_general x1, local copies, waits for them, and re-layouts, shards(): jnp.einsum('bac,hbxc->bhax', flat_blocks, chosen, preferred_element_type=...  7.89 us
    dot_general x1, matrix products, shards(): jnp.einsum('hnab,nshbc->nsac', left_environment, mixed, preferred_element...  6.13 us
    dot_general x1, matrix products, shards(): jnp.einsum('bac,hbxc->bhax', flat_blocks, chosen, preferred_element_type=...  4.66 us
    gather x1, local copies, waits for them, and re-layouts, shards(): chosen = jnp.take(gathered, place_flat, axis=1)  4.34 us
  transfers between devices with their start and end apart: 1, of which 1 were waited for; matrix products, arithmetic and copies ran while one was open for 4% of the time, Pallas kernels for 0%

commit v1 on v0

--- a/solution.py
+++ b/solution.py
@@ -35,7 +35,15 @@
     block_count = sectors * states
     flat_blocks = masked.reshape(block_count, block_rows, block_rows)
     place_flat = lookup(sector_place, sector_ids).reshape(block_count)
-    gathered = lax.all_gather(right_environment, "bond", axis=1, tiled=True)
+    ways, here, lap = (lax.axis_size("bond"), lax.axis_index("bond"), right_environment.shape[1])
+    line, have = (right_environment, 1)
+    while have < ways:
+        line = jnp.concatenate(
+            [line, lax.ppermute(line, "bond", [(d, (d - have) % ways) for d in range(ways)])],
+            axis=1,
+        )
+        have = 2 * have
+    gathered = jnp.roll(line, here * lap, axis=1)
     chosen = jnp.take(gathered, place_flat, axis=1)
     right_part = jnp.einsum(
         "bac,hbxc->bhax", flat_blocks, chosen, preferred_element_type=jnp.float32

time: 173 us -> 179 us (1.035)
  between operations: 13.5 us -> 0.13 us
  starting transfers between devices: 0.04 us -> 8.07 us
  waiting for transfers between devices: 48.3 us -> 55.1 us
  other arithmetic: 4.04 us -> 5.84 us
    ppermute x0 -> x3, waiting for transfers between devices: none -> 55.1 us  [shards(): lax.ppermute(line, 'bond', [(d, (d - have) % ways) for d in range(ways)])]
    all_gather x1 -> x0, waiting for transfers between devices: 47.6 us -> none  [shards(): gathered = lax.all_gather(right_environment, 'bond', axis=1, tiled=True)]
    ppermute x0 -> x3, starting transfers between devices: none -> 8.07 us  [shards(): lax.ppermute(line, 'bond', [(d, (d - have) % ways) for d in range(ways)])]
    unnamed x13 -> x18, local copies, waits for them, and re-layouts: 2.88 us -> 4.13 us
  transfers between devices with their start and end apart: 1 -> 3, of which waited for: 1 -> 3; matrix products, arithmetic and copies ran while one was open for 4% -> 5% of each run, Pallas kernels for 0% -> 0%
where the time goes in v1:
time: 179 us; the launch traced here: 178 us
  blocking collectives  76.1 us (43%)
  waiting for transfers between devices  55.1 us (31%)
  local copies, waits for them, and re-layouts  16.7 us (9%)
  matrix products  15.8 us (9%)
  starting transfers between devices  8.07 us (5%)
  other arithmetic  5.84 us (3%)
    psum x1, blocking collectives, shards(): summed = lax.psum(partial_value, 'mpo')  76.1 us
    ppermute x3, waiting for transfers between devices, shards(): lax.ppermute(line, 'bond', [(d, (d - have) % ways) for d in range(ways)])  55.1 us
    ppermute x3, starting transfers between devices, shards(): lax.ppermute(line, 'bond', [(d, (d - have) % ways) for d in range(ways)])  8.07 us
    dot_general x1, local copies, waits for them, and re-layouts, shards(): jnp.einsum('bac,hbxc->bhax', flat_blocks, chosen, preferred_element_type=...  7.94 us
    dot_general x1, matrix products, shards(): jnp.einsum('bac,hbxc->bhax', flat_blocks, chosen, preferred_element_type=...  6.23 us
    dot_general x1, matrix products, shards(): jnp.einsum('hnab,nshbc->nsac', left_environment, mixed, preferred_element...  6.13 us
    unnamed x18, local copies, waits for them, and re-layouts  4.13 us
  transfers between devices with their start and end apart: 3, of which 3 were waited for; matrix products, arithmetic and copies ran while one was open for 5% of the time, Pallas kernels for 0%

profile of v1, /device:TPU:0, one launch (start us, length us, event | category | flops | bytes accessed | tf_op | source)
XLA Modules:
  0.0 177.7 jit_solution(15616150840104633908)
XLA Ops:
  0.0 0.0 copy-start
  0.0 6.1 %collective-permute-start = (bf16[2,1,256,256]{3,2,1,0:T(8,128)(2,1)}, bf16[2,1,256,256]{3,2,1,0:T(8,128)(2,1)S(1)}, u32[]{:S(2)}, u32[]{:S(2)}) collective-permute-start(bf16[2,1,256,256]{3,2,1,0:T(8,128)(2,1)} %param.10), channel_id=1, source_target_pairs={{0,28},{4,0},{8,4},{12,8},{16,12},{20,16},{24,20},{28,24},{1,29},{... | collective-permute-start | bytes 786440 | tf_op jit(solution)/shard_map/ppermute | solution.py:42
  6.1 0.8 select_reduce_fusion.1
  6.9 5.1 %collective-permute-done = bf16[2,1,256,256]{3,2,1,0:T(8,128)(2,1)S(1)} collective-permute-done((bf16[2,1,256,256]{3,2,1,0:T(8,128)(2,1)}, bf16[2,1,256,256]{3,2,1,0:T(8,128)(2,1)S(1)}, u32[]{:S(2)}, u32[]{:S(2)}) %collective-permute-start) | collective-permute-done | bytes 262176 | tf_op jit(solution)/shard_map/ppermute | solution.py:42
  12.0 1.0 pad_maximum_fusion.1
  13.0 1.5 collective-permute-start.1
  14.5 3.9 %copy.12 = bf16[1,16,256,256]{2,3,1,0:T(8,128)(2,1)} copy(bf16[1,16,256,256]{3,2,1,0:T(8,128)(2,1)} %param.8) | data formatting | bytes 4194304 | tf_op args[0]
  18.4 0.0 copy-done.4
  18.4 0.6 dynamic_slice.13
  19.0 0.0 copy-done.1
  19.0 6.8 %collective-permute-done.1 = bf16[2,2,256,256]{3,2,1,0:T(8,128)(2,1)S(1)} collective-permute-done((bf16[2,2,256,256]{3,2,1,0:T(8,128)(2,1)S(1)}, bf16[2,2,256,256]{3,2,1,0:T(8,128)(2,1)S(1)}, u32[]{:S(2)}, u32[]{:S(2)}) %collective-permute-start.1) | collective-permute-done | bytes 524320 | tf_op jit(solution)/shard_map/ppermute | solution.py:42
  25.8 0.1 pad_maximum_fusion
  25.9 0.5 collective-permute-start.2
  26.4 0.6 iota_compare_fusion.2
  27.1 0.0 copy-done.3
  27.1 0.1 broadcast_compare_fusion
  27.2 0.1 iota_compare_fusion
  27.2 2.0 %broadcast_and_fusion = pred[1,16,256,256]{2,3,1,0:T(8,128)(4,1)} fusion(pred[16,256]{1,0:T(8,128)(4,1)S(1)} %iota_compare_fusion, pred[256]{0:T(512)(128)(4,1)S(1)} %iota_compare_fusion.2), kind=kLoop, calls=%fused_computation.15 | loop fusion | flops 1048576 | bytes 1052928 | tf_op jit(solution)/shard_map/and | solution.py:33
  29.4 43.2 %collective-permute-done.2 = bf16[2,4,256,256]{3,2,1,0:T(8,128)(2,1)S(1)} collective-permute-done((bf16[2,4,256,256]{3,2,1,0:T(8,128)(2,1)S(1)}, bf16[2,4,256,256]{3,2,1,0:T(8,128)(2,1)S(1)}, u32[]{:S(2)}, u32[]{:S(2)}) %collective-permute-start.2) | collective-permute-done | bytes 1048608 | tf_op jit(solution)/shard_map/ppermute | solution.py:42
  72.6 0.1 constant_dynamic-update-slice_fusion.4
  72.7 0.1 constant_dynamic-update-slice_fusion
  72.8 0.2 constant_dynamic-slice_fusion
  73.0 2.8 %gather_fusion = bf16[16,2,256,256]{3,2,1,0:T(8,128)(2,1)} fusion(bf16[2,8,256,256]{3,2,1,0:T(8,128)(2,1)S(1)} %constant_dynamic-slice_fusion, s32[1024]{0:T(1024)S(1)} %pad_clamp_fusion), kind=kCustom, calls=%fused_computation | custom fusion | bytes 8388672 | tf_op jit(solution)/shard_map/jit(_take)/gather | solution.py:47
  75.7 6.2 %fusion.2 = bf16[16,2,256,256]{3,2,1,0:T(8,128)(2,1)} fusion(bf16[16,2,256,256]{3,2,1,0:T(8,128)(2,1)} %gather_fusion, pred[16]{0:T(512)(128)(4,1)S(1)} %compare_and_fusion, bf16[1,16,256,256]{2,3,1,0:T(8,128)(2,1)} %copy.12, pred[16,256]{1,0:T(8,128)(4,1)S(1)} %iota_compare_fusion, pred[256]{0:T(512)(128)(4,1)S(1)} %iota_compare_fusion.2), kind=kOutput, calls=%fused_computation.3 | convolution fusion | flops 1077936128 | bytes 10490128 | tf_op jit(solution)/shard_map/bac,hbxc->bhax/dot_general | solution.py:48
  82.0 7.9 %copy.16 = bf16[16,2,256,256]{2,0,3,1:T(8,128)(2,1)} copy(bf16[16,2,256,256]{3,2,1,0:T(8,128)(2,1)} %fusion.2) | data formatting | bytes 8388608 | tf_op jit(solution)/shard_map/bac,hbxc->bhax/dot_general | solution.py:48
  89.9 0.0 copy-done.2
  89.9 3.4 %convert_bitcast_fusion = bf16[16,2,256,256]{3,0,2,1:T(8,128)(2,1)S(1)} fusion(bf16[16,2,256,256]{2,0,3,1:T(8,128)(2,1)} %copy.16, bf16[2,16,16]{2,1,0:T(8,128)(2,1)S(1)} %copy-done.2, pred[16,16]{1,0:T(8,128)(4,1)S(1)} %broadcast_compare_fusion), kind=kOutput, calls=%fused_computation.8 | convolution fusion | flops 69206528 | bytes 8389888 | tf_op jit(solution)/shard_map/nhst,nthac->nshac/dot_general | solution.py:54
  93.3 0.0 copy-done
  93.4 6.1 %fusion.11 = f32[1,16,256,256]{2,3,1,0:T(8,128)} fusion(bf16[16,2,256,256]{3,0,2,1:T(8,128)(2,1)S(1)} %convert_bitcast_fusion, bf16[2,1,256,256]{3,2,1,0:T(8,128)(2,1)S(1)} %copy-done), kind=kOutput, calls=%fused_computation.11 | convolution fusion | flops 1073741824 | bytes 8650752 | tf_op jit(solution)/shard_map/hnab,nshbc->nsac/dot_general | solution.py:57
  99.5 76.1 %all-reduce.1 = bf16[1,16,256,256]{2,3,1,0:T(8,128)(2,1)S(1)} all-reduce(f32[1,16,256,256]{2,3,1,0:T(8,128)} %fusion.11), channel_id=1, replica_groups=mesh['bond'=8,'mpo'=4] {'mpo'}, use_global_device_ids=true, to_apply=%region_2.3 | all-reduce | flops 1048576 | bytes 6291456 | tf_op jit(solution)/shard_map/psum | solution.py:62
  175.6 1.1 select_convert_fusion
  176.7 1.0 copy.14
  (13 shorter events, 0.2 us)
Async XLA Ops:
  0.0 93.3 %copy-start = (bf16[2,1,256,256]{3,2,1,0:T(8,128)(2,1)S(1)}, bf16[2,1,256,256]{3,2,1,0:T(8,128)(2,1)}, u32[]{:S(2)}) copy-start(bf16[2,1,256,256]{3,2,1,0:T(8,128)(2,1)} %param.9) | copy-start | bytes 786436
  0.0 19.0 %copy-start.1 = (bf16[2,1,256,256]{3,2,1,0:T(8,128)(2,1)S(1)}, bf16[2,1,256,256]{3,2,1,0:T(8,128)(2,1)}, u32[]{:S(2)}) copy-start(bf16[2,1,256,256]{3,2,1,0:T(8,128)(2,1)} %param.10) | copy-start | bytes 786436
  0.0 27.1 %copy-start.3 = (s32[1,16,1]{1,2,0:T(1,128)S(1)}, s32[1,16,1]{1,2,0:T(1,128)}, u32[]{:S(2)}) copy-start(s32[1,16,1]{1,2,0:T(1,128)} %param.12) | copy-start | bytes 196
  0.0 18.4 %copy-start.4 = (s32[8]{0:T(128)S(1)}, s32[8]{0:T(128)}, u32[]{:S(2)}) copy-start(s32[8]{0:T(128)} %param.13) | copy-start | bytes 100
  0.0 11.9 %collective-permute-start = (bf16[2,1,256,256]{3,2,1,0:T(8,128)(2,1)}, bf16[2,1,256,256]{3,2,1,0:T(8,128)(2,1)S(1)}, u32[]{:S(2)}, u32[]{:S(2)}) collective-permute-start(bf16[2,1,256,256]{3,2,1,0:T(8,128)(2,1)} %param.10), channel_id=1, source_target_pairs={{0,28},{4,0},{8,4},{12,8},{16,12},{20,16},{24,20},{28,24},{1,29},{... | collective-permute-start | bytes 786440 | tf_op jit(solution)/shard_map/ppermute | solution.py:42
  13.0 12.9 %collective-permute-start.1 = (bf16[2,2,256,256]{3,2,1,0:T(8,128)(2,1)S(1)}, bf16[2,2,256,256]{3,2,1,0:T(8,128)(2,1)S(1)}, u32[]{:S(2)}, u32[]{:S(2)}) collective-permute-start(bf16[2,2,256,256]{3,2,1,0:T(8,128)(2,1)S(1)} %pad_maximum_fusion.1), channel_id=1, source_target_pairs={{0,24},{4,28},{8,0},{12,4},{16,8},{20,12},{24,16},{28,20},{1,25},{... | collective-permute-start | bytes 1572872 | tf_op jit(solution)/shard_map/ppermute | solution.py:42
  25.9 46.6 %collective-permute-start.2 = (bf16[2,4,256,256]{3,2,1,0:T(8,128)(2,1)S(1)}, bf16[2,4,256,256]{3,2,1,0:T(8,128)(2,1)S(1)}, u32[]{:S(2)}, u32[]{:S(2)}) collective-permute-start(bf16[2,4,256,256]{3,2,1,0:T(8,128)(2,1)S(1)} %pad_maximum_fusion), channel_id=1, source_target_pairs={{0,16},{4,20},{8,24},{12,28},{16,0},{20,4},{24,8},{28,12},{1,17},{... | collective-permute-start | bytes 3145736 | tf_op jit(solution)/shard_map/ppermute | solution.py:42
  82.0 7.9 %copy-start.2 = (bf16[2,16,16]{2,1,0:T(8,128)(2,1)S(1)}, bf16[2,16,16]{2,1,0:T(8,128)(2,1)}, u32[]{:S(2)}) copy-start(bf16[2,16,16]{2,1,0:T(8,128)(2,1)} %param.11) | copy-start | bytes 3076
